TPU v7x, 32 devices: a whole 2x2x4 slice. The times are simulated.
32 devices in a mesh: feat: 8 (over z, y), tok: 4 (over x, core).
Axes of the slice: x: 2, y: 2, z: 4, core: 2. Of those that a mesh axis runs over, the one named last changes fastest.
Arguments:
- activations: bfloat16 [2048, 7168], P('tok', 'feat'), may hold values from -6 to 6
- top_lists: int32 [2048, 64], P('tok'), may hold values from 0 to 4095, all different within a row
- encoder_weight: bfloat16 [7168, 4096], P(None, 'feat'), may hold values from -0.0625 to 0.0625
- encoder_bias: float32 [4096], P('feat'), may hold values from -3 to 3
- decoder_weight: bfloat16 [7168, 4096], P(None, 'feat'), may hold values from -0.125 to 0.125
- decoder_bias: float32 [7168], replicated, may hold values from -3 to 3
Outputs:
- encoder_grad: float32 [7168, 4096], P('tok', 'feat')
- decoder_grad: float32 [7168, 4096], P('tok', 'feat')
All inputs are finite; a program needn't handle non-finite values.
Results may differ from a plain program's by a relative error of at most 0.004.
Values may be sent and summed in bfloat16 or wider, within the bound.
A program may use at most 128 MiB of HBM per device.

v0:
```python
import jax
import jax.numpy as jnp
from jax import lax
from jax.sharding import PartitionSpec as P


def contract_rows(left, right):
    return lax.dot_general(
        left, right, (((0,), (0,)), ((), ())), preferred_element_type=jnp.float32
    )


def body(activations, top_lists, encoder_weight, encoder_bias, decoder_weight, decoder_bias):
    group_rows = activations.shape[0]
    feat_dev = encoder_weight.shape[1]
    shards = lax.axis_size("feat")
    owner = lax.axis_index("feat")
    row_share = group_rows // shards
    gathered = lax.all_gather(activations, "feat", axis=1, tiled=True)
    encoded = jnp.dot(gathered, encoder_weight, preferred_element_type=jnp.float32) + encoder_bias
    local_ids = top_lists - owner * feat_dev
    inside = (local_ids >= 0) & (local_ids < feat_dev)
    column = jnp.where(inside, local_ids, feat_dev)
    row_ids = jnp.arange(group_rows, dtype=jnp.int32)[:, None]
    chosen = (
        jnp.zeros((group_rows, feat_dev), jnp.float32).at[row_ids, column].set(1.0, mode="drop")
    )
    codes = jnp.where(chosen > 0.0, encoded, 0.0).astype(jnp.bfloat16)
    rebuilt = lax.psum_scatter(
        lax.dot_general(
            codes, decoder_weight, (((1,), (1,)), ((), ())), preferred_element_type=jnp.float32
        ),
        "feat",
        scatter_dimension=0,
        tiled=True,
    )
    own_rows = lax.dynamic_slice_in_dim(gathered, owner * row_share, row_share, 0)
    error_rows = (rebuilt + decoder_bias - own_rows.astype(jnp.float32)).astype(jnp.bfloat16)
    error = lax.all_gather(error_rows, "feat", axis=0, tiled=True)
    pulled = jnp.dot(error, decoder_weight, preferred_element_type=jnp.float32)
    code_grads = jnp.where(chosen > 0.0, pulled, 0.0).astype(jnp.bfloat16)
    input_cols, error_cols = (
        lax.all_to_all(gathered, "tok", split_axis=1, concat_axis=0, tiled=True),
        lax.all_to_all(error, "tok", split_axis=1, concat_axis=0, tiled=True),
    )
    grads_all, codes_all = (
        lax.all_gather(code_grads, "tok", axis=0, tiled=True),
        lax.all_gather(codes, "tok", axis=0, tiled=True),
    )
    encoder_grad = contract_rows(input_cols, grads_all)
    decoder_grad = contract_rows(error_cols, codes_all)
    return (encoder_grad, decoder_grad)


def solution(mesh):
    return jax.shard_map(
        body,
        mesh=mesh,
        in_specs=(
            P("tok", "feat"),
            P("tok", None),
            P(None, "feat"),
            P("feat"),
            P(None, "feat"),
            P(),
        ),
        out_specs=(P("tok", "feat"), P("tok", "feat")),
        check_vma=False,
    )
```

profile of v0, /device:TPU:0, one launch (start us, length us, event | category | flops | bytes accessed | tf_op | source)
XLA Modules:
  0.0 639.1 jit_solution(12103646338569349608)
XLA Ops:
  7.2 0.0 all-gather.5.cloned.1.call-start
  7.2 0.7 all-gather.5.cloned.1.call-update
  7.9 0.0 reduce-scatter.2.cloned.1.call-start
  7.9 0.9 fusion.5
  8.9 0.1 and_reduce_fusion
  9.0 0.8 multiply_reduce_fusion
  9.8 0.1 copy.12
  9.9 0.1 reshape.20
  10.0 120.3 %scatter_custom_fusion = f32[262144]{0:T(1024)S(1)} fusion(s32[32768]{0:T(1024)S(1)} %reshape.20, f32[32768]{0:T(1024)S(1)} %broadcast.30, f32[]{:T(128)} %constant.7.clone.1), kind=kCustom, calls=%fused_computation.11 | custom fusion | bytes 1048580
  130.3 0.1 broadcast_compare_fusion
  130.5 0.4 reshape.19
  130.8 0.0 all-gather.5.cloned.1.call-done
  130.9 9.1 %fusion.1 = bf16[512,512]{1,0:T(8,128)(2,1)S(1)} fusion(pred[512,512]{1,0:T(32,128)(4,1)S(1)} %reshape.19, bf16[512,7168]{1,0:T(8,128)(2,1)} %all-gather.5.cloned.1.call-done, bf16[7168,512]{1,0:T(8,128)(2,1)} %param.8, f32[512]{0:T(512)} %param.9), kind=kOutput, calls=%fused_computation.8 | convolution fusion | flops 3758882816 | bytes 15468544 | tf_op jit(solution)/shard_map/dot_general | solution.py:20
  140.0 0.0 copy-start
  140.0 10.5 %fusion.6 = f32[512,7168]{1,0:T(8,128)} fusion(bf16[512,512]{1,0:T(8,128)(2,1)S(1)} %fusion.1, bf16[7168,512]{1,0:T(8,128)(2,1)} %param.10), kind=kOutput, calls=%fused_computation.19 | convolution fusion | flops 3758096384 | bytes 22544384 | tf_op jit(solution)/shard_map/dot_general | solution.py:30
  150.5 0.0 copy-done
  150.5 0.0 copy-start.1
  150.5 0.0 reduce-scatter.2.cloned.1.call-update
  150.6 0.0 all-gather.7.cloned.1.call-start
  150.6 239.5 %reduce-scatter.2.cloned.1.call-done = f32[64,7168]{1,0:T(8,128)} async-done(((f32[512,7168]{1,0:T(8,128)}), f32[64,7168]{1,0:T(8,128)}) %reduce-scatter.2.cloned.1.call-update) | async-done | bytes 1835024 | tf_op jit(solution)/shard_map/reduce_scatter | solution.py:29
  390.1 0.0 copy-done.1
  390.1 2.9 subtract_convert_fusion
  393.0 0.0 all-gather.7.cloned.1.call-update
  393.0 6.6 %copy.21 = bf16[64,4,8,1792]{3,2,0,1:T(8,128)(2,1)} copy(bf16[64,4,8,1792]{3,2,1,0:T(8,128)(2,1)} %bitcast.30) | data formatting | bytes 14680064 | tf_op jit(solution)/shard_map/all_to_all | solution.py:43
  399.6 5.7 all-to-all-start
  405.3 0.0 all-gather.9.cloned.1.call-start
  405.4 98.4 %all-gather.7.cloned.1.call-done = bf16[512,7168]{1,0:T(8,128)(2,1)} async-done(((bf16[64,7168]{1,0:T(8,128)(2,1)}), bf16[512,7168]{1,0:T(8,128)(2,1)}) %all-gather.7.cloned.1.call-update) | async-done | bytes 7340048 | tf_op jit(solution)/shard_map/all_gather | solution.py:39
  503.8 9.9 %fusion.2 = bf16[512,512]{1,0:T(8,128)(2,1)} fusion(pred[512,512]{1,0:T(32,128)(4,1)S(1)} %reshape.19, bf16[512,7168]{1,0:T(8,128)(2,1)} %all-gather.7.cloned.1.call-done, bf16[7168,512]{1,0:T(8,128)(2,1)} %param.10), kind=kOutput, calls=%fused_computation.9 | convolution fusion | flops 3758620672 | bytes 15466496 | tf_op jit(solution)/shard_map/dot_general | solution.py:40
  513.7 0.0 all-gather.9.cloned.1.call-update
  513.7 6.6 %copy.20 = bf16[64,4,8,1792]{3,2,0,1:T(8,128)(2,1)} copy(bf16[64,4,8,1792]{3,2,1,0:T(8,128)(2,1)} %bitcast.31) | data formatting | bytes 14680064 | tf_op jit(solution)/shard_map/all_to_all | solution.py:44
  520.3 0.0 all-to-all-done
  520.3 5.4 all-to-all-start.1
  525.8 0.2 all-gather.11.cloned.1.call-start
  526.0 0.4 all-gather.11.cloned.1.call-update
  526.4 12.4 %all-gather.9.cloned.1.call-done = bf16[2048,512]{1,0:T(8,128)(2,1)} async-done(((bf16[512,512]{1,0:T(8,128)(2,1)}), bf16[2048,512]{1,0:T(8,128)(2,1)}) %all-gather.9.cloned.1.call-update) | async-done | bytes 2097168 | tf_op jit(solution)/shard_map/all_gather | solution.py:47
  538.8 9.6 %convolution_bitcast_fusion = f32[1792,512]{0,1:T(8,128)} fusion(bf16[2048,512]{1,0:T(8,128)(2,1)} %all-gather.9.cloned.1.call-done, bf16[2048,1792]{1,0:T(8,128)(2,1)} %bitcast.2), kind=kOutput, calls=%fused_computation.3 | convolution fusion | flops 3758096384 | bytes 13107200 | tf_op jit(solution)/shard_map/dot_general | solution.py:8
  548.4 5.2 copy.15
  553.6 23.4 %all-gather.11.cloned.1.call-done = bf16[2048,512]{1,0:T(8,128)(2,1)} async-done(((bf16[512,512]{1,0:T(8,128)(2,1)}), bf16[2048,512]{1,0:T(8,128)(2,1)}) %all-gather.11.cloned.1.call-update) | async-done | bytes 2097168 | tf_op jit(solution)/shard_map/all_gather | solution.py:48
  577.0 46.0 %all-to-all-done.1 = bf16[512,4,1792]{2,0,1:T(8,128)(2,1)} async-done(((bf16[512,4,1792]{2,0,1:T(8,128)(2,1)}), bf16[512,4,1792]{2,0,1:T(8,128)(2,1)}, u32[]{:S(2)}, u32[]{:S(2)}) %all-to-all-start.1) | async-done | bytes 7340064 | tf_op jit(solution)/shard_map/all_to_all | solution.py:44
  623.1 9.5 %fusion.7 = f32[1792,512]{1,0:T(8,128)} fusion(bf16[2048,1792]{1,0:T(8,128)(2,1)} %bitcast.5, bf16[2048,512]{1,0:T(8,128)(2,1)} %all-gather.11.cloned.1.call-done), kind=kOutput, calls=%fused_computation.20 | convolution fusion | flops 3758096384 | bytes 13107200 | tf_op jit(solution)/shard_map/dot_general | solution.py:8
  (3 shorter events, 0.0 us)
Async XLA Ops:
  7.2 123.7 %all-gather.5.cloned.1.call-start = ((), (), s32[]{:S(2)}) async-start(), calls=%async_computation.3 | async-start | bytes 8257536 | tf_op jit(solution)/shard_map/all_gather | solution.py:19
  7.9 382.2 %reduce-scatter.2.cloned.1.call-start = ((), (), s32[]{:S(2)}) async-start(), calls=%async_computation.4 | async-start | bytes 16515072 | tf_op jit(solution)/shard_map/reduce_scatter | solution.py:29
  140.0 10.5 %copy-start = (bf16[512,512]{1,0:T(8,128)(2,1)}, bf16[512,512]{1,0:T(8,128)(2,1)S(1)}, u32[]{:S(2)}) copy-start(bf16[512,512]{1,0:T(8,128)(2,1)S(1)} %fusion.1) | copy-start | bytes 1572868
  150.5 239.6 %copy-start.1 = (f32[7168]{0:T(1024)S(1)}, f32[7168]{0:T(1024)}, u32[]{:S(2)}) copy-start(f32[7168]{0:T(1024)} %param.11) | copy-start | bytes 86020
  150.6 353.2 %all-gather.7.cloned.1.call-start = ((), (), s32[]{:S(2)}) async-start(), calls=%async_computation.5 | async-start | bytes 8257536 | tf_op jit(solution)/shard_map/all_gather | solution.py:39
  399.6 120.8 %all-to-all-start = ((bf16[512,4,1792]{2,0,1:T(8,128)(2,1)}), bf16[512,4,1792]{2,0,1:T(8,128)(2,1)}, u32[]{:S(2)}, u32[]{:S(2)}) async-start(bf16[512,4,1792]{2,0,1:T(8,128)(2,1)} %bitcast.29), calls=%async_computation.1 | async-start | bytes 14680064 | tf_op jit(solution)/shard_map/all_to_all | solution.py:43
  405.3 133.5 %all-gather.9.cloned.1.call-start = ((), (), s32[]{:S(2)}) async-start(), calls=%async_computation.6 | async-start | bytes 2621440 | tf_op jit(solution)/shard_map/all_gather | solution.py:47
  520.3 102.7 %all-to-all-start.1 = ((bf16[512,4,1792]{2,0,1:T(8,128)(2,1)}), bf16[512,4,1792]{2,0,1:T(8,128)(2,1)}, u32[]{:S(2)}, u32[]{:S(2)}) async-start(bf16[512,4,1792]{2,0,1:T(8,128)(2,1)} %bitcast.28), calls=%async_computation.2 | async-start | bytes 14680064 | tf_op jit(solution)/shard_map/all_to_all | solution.py:44
  525.8 51.2 %all-gather.11.cloned.1.call-start = ((), (), s32[]{:S(2)}) async-start(), calls=%async_computation.7 | async-start | bytes 2621440 | tf_op jit(solution)/shard_map/all_gather | solution.py:48
Sparse Core Ops, SparseCore 0:
  10.2 113.9 all-gather.4
  150.7 239.3 reduce-scatter.1
  393.1 110.5 all-gather.6
  513.8 24.9 all-gather.8
  540.2 36.7 all-gather.10
where the time goes:
time: 640 us; the launch traced here: 639 us
  waiting for transfers between devices  421 us (66%)
  local copies, waits for them, and re-layouts  139 us (22%)
  matrix products  48.7 us (8%)
  between operations  13.9 us (2%)
  starting transfers between devices  11.5 us (2%)
    reduce_scatter x1, waiting for transfers between devices, body(): lax.psum_scatter(lax.dot_general(codes, decoder_weight, (((1,), (1,)), ((...  240 us
    unnamed x9, local copies, waits for them, and re-layouts  126 us
    all_gather x1, waiting for transfers between devices, body(): error = lax.all_gather(error_rows, 'feat', axis=0, tiled=True)  98.4 us
    all_to_all x1, waiting for transfers between devices, body(): lax.all_to_all(error, 'tok', split_axis=1, concat_axis=0, tiled=True)  46 us
    all_gather x1, waiting for transfers between devices, body(): lax.all_gather(codes, 'tok', axis=0, tiled=True)  23.4 us
    dot_general x2, matrix products, contract_rows(): lax.dot_general(left, right, (((0,), (0,)), ((), ())), preferred_element_...  19.1 us
  transfers between devices with their start and end apart: 7, of which 5 were waited for; matrix products, arithmetic and copies ran while one was open for 25% of the time, Pallas kernels for 0%

commit v1 on v0

--- a/solution.py
+++ b/solution.py
@@ -36,7 +36,14 @@
     )
     own_rows = lax.dynamic_slice_in_dim(gathered, owner * row_share, row_share, 0)
     error_rows = (rebuilt + decoder_bias - own_rows.astype(jnp.float32)).astype(jnp.bfloat16)
-    error = lax.all_gather(error_rows, "feat", axis=0, tiled=True)
+    size = lax.axis_size("feat")
+    forward = [(i, (i + 1) % size) for i in range(size)]
+    parts = [error_rows]
+    for far in range(1, size):
+        parts = [lax.ppermute(parts[0], "feat", forward), *parts]
+    full = jnp.concatenate(parts, axis=0)
+    places = (lax.axis_index("feat") + 1) * parts[-1].shape[0]
+    error = jnp.roll(full, places, axis=0)
     pulled = jnp.dot(error, decoder_weight, preferred_element_type=jnp.float32)
     code_grads = jnp.where(chosen > 0.0, pulled, 0.0).astype(jnp.bfloat16)
     input_cols, error_cols = (

time: 640 us -> 762 us (1.19)
  waiting for transfers between devices: 421 us -> 497 us
  local copies, waits for them, and re-layouts: 139 us -> 187 us
    ppermute x0 -> x7, waiting for transfers between devices: none -> 142 us  [body(): parts = [lax.ppermute(parts[0], 'feat', forward), *parts]]
    all_gather x1 -> x0, waiting for transfers between devices: 98.4 us -> none  [body(): error = lax.all_gather(error_rows, 'feat', axis=0, tiled=True)]
    all_to_all x1, waiting for transfers between devices: 0.01 us -> 36.7 us  [body(): lax.all_to_all(gathered, 'tok', split_axis=1, concat_axis=0, tiled=True)]
    all_to_all x1, waiting for transfers between devices: 46 us -> 77.7 us  [body(): lax.all_to_all(error, 'tok', split_axis=1, concat_axis=0, tiled=True)]
    unnamed x9 -> x38, local copies, waits for them, and re-layouts: 126 us -> 155 us
    all_gather x1, waiting for transfers between devices: 23.4 us -> 0.01 us  [body(): lax.all_gather(codes, 'tok', axis=0, tiled=True)]
    dynamic_slice x0 -> x2, local copies, waits for them, and re-layouts: none -> 14 us  [body(): error = jnp.roll(full, places, axis=0)]
    all_gather x1, waiting for transfers between devices: 12.4 us -> 0.02 us  [body(): lax.all_gather(code_grads, 'tok', axis=0, tiled=True)]
  transfers between devices with their start and end apart: 7 -> 13, of which waited for: 5 -> 10; matrix products, arithmetic and copies ran while one was open for 25% -> 26% of each run, Pallas kernels for 0% -> 0%
where the time goes in v1:
time: 762 us; the launch traced here: 760 us
  waiting for transfers between devices  497 us (65%)
  local copies, waits for them, and re-layouts  187 us (25%)
  matrix products  45.9 us (6%)
  between operations  14 us (2%)
  starting transfers between devices  12.8 us (2%)
    reduce_scatter x1, waiting for transfers between devices, body(): lax.psum_scatter(lax.dot_general(codes, decoder_weight, (((1,), (1,)), ((...  240 us
    unnamed x38, local copies, waits for them, and re-layouts  155 us
    ppermute x7, waiting for transfers between devices, body(): parts = [lax.ppermute(parts[0], 'feat', forward), *parts]  142 us
    all_to_all x1, waiting for transfers between devices, body(): lax.all_to_all(error, 'tok', split_axis=1, concat_axis=0, tiled=True)  77.7 us
    all_to_all x1, waiting for transfers between devices, body(): lax.all_to_all(gathered, 'tok', split_axis=1, concat_axis=0, tiled=True)  36.7 us
    dot_general x2, matrix products, contract_rows(): lax.dot_general(left, right, (((0,), (0,)), ((), ())), preferred_element_...  19.1 us
  transfers between devices with their start and end apart: 13, of which 10 were waited for; matrix products, arithmetic and copies ran while one was open for 26% of the time, Pallas kernels for 0%

profile of v1, /device:TPU:0, one launch (start us, length us, event | category | flops | bytes accessed | tf_op | source)
XLA Modules:
  0.0 760.4 jit_solution(14447818664293799185)
XLA Ops:
  7.2 0.0 all-gather.4.cloned.1.call-start
  7.2 0.7 all-gather.4.cloned.1.call-update
  7.9 0.0 reduce-scatter.2.cloned.1.call-start
  7.9 0.9 fusion.5
  8.9 0.1 and_reduce_fusion
  9.0 0.8 multiply_reduce_fusion
  9.8 0.1 copy.15
  9.9 0.1 reshape.20
  10.0 120.3 %scatter_custom_fusion = f32[262144]{0:T(1024)S(1)} fusion(s32[32768]{0:T(1024)S(1)} %reshape.20, f32[32768]{0:T(1024)S(1)} %broadcast.31, f32[]{:T(128)} %constant.16.clone.1), kind=kCustom, calls=%fused_computation.10 | custom fusion | bytes 1048580
  130.3 0.1 broadcast_compare_fusion
  130.5 0.4 reshape.19
  130.8 0.0 all-gather.4.cloned.1.call-done
  130.9 9.1 %fusion.1 = bf16[512,512]{1,0:T(8,128)(2,1)S(1)} fusion(pred[512,512]{1,0:T(32,128)(4,1)S(1)} %reshape.19, bf16[512,7168]{1,0:T(8,128)(2,1)} %all-gather.4.cloned.1.call-done, bf16[7168,512]{1,0:T(8,128)(2,1)} %param.8, f32[512]{0:T(512)} %param.9), kind=kOutput, calls=%fused_computation.7 | convolution fusion | flops 3758882816 | bytes 15468544 | tf_op jit(solution)/shard_map/dot_general | solution.py:20
  140.0 0.0 copy-start.8
  140.0 10.6 %fusion.6 = f32[512,7168]{1,0:T(8,128)} fusion(bf16[512,512]{1,0:T(8,128)(2,1)S(1)} %fusion.1, bf16[7168,512]{1,0:T(8,128)(2,1)} %param.10), kind=kOutput, calls=%fused_computation.35 | convolution fusion | flops 3758096384 | bytes 22544384 | tf_op jit(solution)/shard_map/dot_general | solution.py:30
  150.6 0.0 reduce-scatter.2.cloned.1.call-update
  150.7 239.5 %reduce-scatter.2.cloned.1.call-done = f32[64,7168]{1,0:T(8,128)} async-done(((f32[512,7168]{1,0:T(8,128)}), f32[64,7168]{1,0:T(8,128)}) %reduce-scatter.2.cloned.1.call-update) | async-done | bytes 1835024 | tf_op jit(solution)/shard_map/reduce_scatter | solution.py:29
  390.2 1.9 subtract_convert_fusion
  392.1 1.5 collective-permute-start
  393.6 23.2 %collective-permute-done = bf16[64,7168]{1,0:T(8,128)(2,1)S(1)} collective-permute-done((bf16[64,7168]{1,0:T(8,128)(2,1)S(1)}, bf16[64,7168]{1,0:T(8,128)(2,1)S(1)}, u32[]{:S(2)}, u32[]{:S(2)}) %collective-permute-start) | collective-permute-done | bytes 917536 | tf_op jit(solution)/shard_map/ppermute | solution.py:43
  416.9 23.9 %collective-permute-done.1 = bf16[64,7168]{1,0:T(8,128)(2,1)S(1)} collective-permute-done((bf16[64,7168]{1,0:T(8,128)(2,1)S(1)}, bf16[64,7168]{1,0:T(8,128)(2,1)S(1)}, u32[]{:S(2)}, u32[]{:S(2)}) %collective-permute-start.1) | collective-permute-done | bytes 917536 | tf_op jit(solution)/shard_map/ppermute | solution.py:43
  440.8 23.0 %collective-permute-done.2 = bf16[64,7168]{1,0:T(8,128)(2,1)S(1)} collective-permute-done((bf16[64,7168]{1,0:T(8,128)(2,1)S(1)}, bf16[64,7168]{1,0:T(8,128)(2,1)S(1)}, u32[]{:S(2)}, u32[]{:S(2)}) %collective-permute-start.2) | collective-permute-done | bytes 917536 | tf_op jit(solution)/shard_map/ppermute | solution.py:43
  463.8 1.0 copy-done.1
  464.8 22.1 %collective-permute-done.3 = bf16[64,7168]{1,0:T(8,128)(2,1)S(1)} collective-permute-done((bf16[64,7168]{1,0:T(8,128)(2,1)S(1)}, bf16[64,7168]{1,0:T(8,128)(2,1)S(1)}, u32[]{:S(2)}, u32[]{:S(2)}) %collective-permute-start.3) | collective-permute-done | bytes 917536 | tf_op jit(solution)/shard_map/ppermute | solution.py:43
  486.9 0.9 copy-done.3
  487.8 21.3 %collective-permute-done.4 = bf16[64,7168]{1,0:T(8,128)(2,1)S(1)} collective-permute-done((bf16[64,7168]{1,0:T(8,128)(2,1)S(1)}, bf16[64,7168]{1,0:T(8,128)(2,1)S(1)}, u32[]{:S(2)}, u32[]{:S(2)}) %collective-permute-start.4) | collective-permute-done | bytes 917536 | tf_op jit(solution)/shard_map/ppermute | solution.py:43
  509.1 0.9 copy-done.5
  510.0 20.5 %collective-permute-done.5 = bf16[64,7168]{1,0:T(8,128)(2,1)} collective-permute-done((bf16[64,7168]{1,0:T(8,128)(2,1)S(1)}, bf16[64,7168]{1,0:T(8,128)(2,1)}, u32[]{:S(2)}, u32[]{:S(2)}) %collective-permute-start.5) | collective-permute-done | bytes 917536 | tf_op jit(solution)/shard_map/ppermute | solution.py:43
  530.6 6.5 copy.22
  537.1 5.4 all-to-all-start
  542.5 0.0 all-gather.6.cloned.1.call-start
  542.6 0.0 copy-start.4
  542.6 7.9 %collective-permute-done.6 = bf16[64,7168]{1,0:T(8,128)(2,1)} collective-permute-done((bf16[64,7168]{1,0:T(8,128)(2,1)}, bf16[64,7168]{1,0:T(8,128)(2,1)}, u32[]{:S(2)}, u32[]{:S(2)}) %collective-permute-start.6) | collective-permute-done | bytes 917536 | tf_op jit(solution)/shard_map/ppermute | solution.py:43
  550.5 2.2 constant_dynamic-update-slice_fusion.15
  552.6 2.2 constant_dynamic-update-slice_fusion.14
  554.9 2.2 constant_dynamic-update-slice_fusion.13
  557.0 2.2 constant_dynamic-update-slice_fusion.12
  559.2 2.2 constant_dynamic-update-slice_fusion.11
  561.4 1.0 constant_dynamic-update-slice_fusion.10
  562.4 1.0 constant_dynamic-update-slice_fusion.9
  563.4 1.0 constant_dynamic-update-slice_fusion.8
  564.4 2.2 constant_dynamic-update-slice_fusion.7
  566.6 2.2 constant_dynamic-update-slice_fusion.6
  568.8 1.0 constant_dynamic-update-slice_fusion.5
  569.8 1.0 constant_dynamic-update-slice_fusion.4
  570.8 1.0 constant_dynamic-update-slice_fusion.3
  571.8 1.0 constant_dynamic-update-slice_fusion.2
  572.8 1.0 constant_dynamic-update-slice_fusion.1
  573.8 1.0 constant_dynamic-update-slice_fusion
  574.8 3.6 constant_dynamic-slice_fusion
  578.4 3.0 copy-done
  581.4 7.1 fusion.2
  588.5 0.0 all-gather.6.cloned.1.call-update
  588.5 10.5 %copy.17 = bf16[512,7168]{0,1:T(8,128)(2,1)} copy(bf16[512,7168]{1,0:T(8,128)(2,1)} %copy-done) | data formatting | bytes 14680064 | tf_op jit(solution)/shard_map/jit(_roll_dynamic)/dynamic_slice | solution.py:46
  599.0 36.7 %all-to-all-done = bf16[512,4,1792]{2,0,1:T(8,128)(2,1)} async-done(((bf16[512,4,1792]{2,0,1:T(8,128)(2,1)}), bf16[512,4,1792]{2,0,1:T(8,128)(2,1)}, u32[]{:S(2)}, u32[]{:S(2)}) %all-to-all-start) | async-done | bytes 7340064 | tf_op jit(solution)/shard_map/all_to_all | solution.py:50
  635.7 5.5 all-to-all-start.1
  641.2 0.2 all-gather.8.cloned.1.call-start
  641.4 0.3 all-gather.8.cloned.1.call-update
  641.7 0.0 all-gather.6.cloned.1.call-done
  641.8 9.6 %convolution_bitcast_fusion = f32[1792,512]{0,1:T(8,128)} fusion(bf16[2048,512]{1,0:T(8,128)(2,1)} %all-gather.6.cloned.1.call-done, bf16[2048,1792]{1,0:T(8,128)(2,1)} %bitcast.2), kind=kOutput, calls=%fused_computation.2 | convolution fusion | flops 3758096384 | bytes 13107200 | tf_op jit(solution)/shard_map/dot_general | solution.py:8
  651.4 5.2 copy.19
  656.6 77.7 %all-to-all-done.1 = bf16[512,4,1792]{0,2,1:T(8,128)(2,1)} async-done(((bf16[512,4,1792]{0,2,1:T(8,128)(2,1)}), bf16[512,4,1792]{0,2,1:T(8,128)(2,1)}, u32[]{:S(2)}, u32[]{:S(2)}) %all-to-all-start.1) | async-done | bytes 7340064 | tf_op jit(solution)/shard_map/all_to_all | solution.py:51
  734.3 10.0 %copy.18 = bf16[4,512,1792]{2,1,0:T(8,128)(2,1)} copy(bf16[4,512,1792]{1,2,0:T(8,128)(2,1)} %bitcast.5) | data formatting | bytes 14680064 | tf_op jit(solution)/shard_map/all_to_all | solution.py:51
  744.3 9.5 %fusion.7 = f32[1792,512]{1,0:T(8,128)} fusion(bf16[2048,1792]{1,0:T(8,128)(2,1)} %bitcast.27, bf16[2048,512]{1,0:T(8,128)(2,1)} %all-gather.8.cloned.1.call-done), kind=kOutput, calls=%fused_computation.36 | convolution fusion | flops 3758096384 | bytes 13107200 | tf_op jit(solution)/shard_map/dot_general | solution.py:8
  (22 shorter events, 0.1 us)
Async XLA Ops:
  7.2 123.7 %all-gather.4.cloned.1.call-start = ((), (), s32[]{:S(2)}) async-start(), calls=%async_computation.3 | async-start | bytes 8257536 | tf_op jit(solution)/shard_map/all_gather | solution.py:19
  7.9 382.3 %reduce-scatter.2.cloned.1.call-start = ((), (), s32[]{:S(2)}) async-start(), calls=%async_computation.4 | async-start | bytes 16515072 | tf_op jit(solution)/shard_map/reduce_scatter | solution.py:29
  140.0 10.6 %copy-start.7 = (bf16[512,512]{1,0:T(8,128)(2,1)}, bf16[512,512]{1,0:T(8,128)(2,1)S(1)}, u32[]{:S(2)}) copy-start(bf16[512,512]{1,0:T(8,128)(2,1)S(1)} %fusion.1) | copy-start | bytes 1572868
  140.0 250.2 %copy-start.8 = (f32[7168]{0:T(1024)S(1)}, f32[7168]{0:T(1024)}, u32[]{:S(2)}) copy-start(f32[7168]{0:T(1024)} %param.11) | copy-start | bytes 86020
  392.1 24.8 %collective-permute-start = (bf16[64,7168]{1,0:T(8,128)(2,1)S(1)}, bf16[64,7168]{1,0:T(8,128)(2,1)S(1)}, u32[]{:S(2)}, u32[]{:S(2)}) collective-permute-start(bf16[64,7168]{1,0:T(8,128)(2,1)S(1)} %subtract_convert_fusion), channel_id=1, source_target_pairs={{0,4},{4,8},{8,12},{12,16},{16,20},{20,24},{24,28},{28,0},{1,5},{5... | collective-permute-start | bytes 2752520 | tf_op jit(solution)/shard_map/ppermute | solution.py:43
  416.9 23.9 %collective-permute-start.1 = (bf16[64,7168]{1,0:T(8,128)(2,1)S(1)}, bf16[64,7168]{1,0:T(8,128)(2,1)S(1)}, u32[]{:S(2)}, u32[]{:S(2)}) collective-permute-start(bf16[64,7168]{1,0:T(8,128)(2,1)S(1)} %collective-permute-done), channel_id=1, source_target_pairs={{0,4},{4,8},{8,12},{12,16},{16,20},{20,24},{24,28},{28,0},{1,5},{5... | collective-permute-start | bytes 2752520 | tf_op jit(solution)/shard_map/ppermute | solution.py:43
  440.8 23.0 %collective-permute-start.2 = (bf16[64,7168]{1,0:T(8,128)(2,1)S(1)}, bf16[64,7168]{1,0:T(8,128)(2,1)S(1)}, u32[]{:S(2)}, u32[]{:S(2)}) collective-permute-start(bf16[64,7168]{1,0:T(8,128)(2,1)S(1)} %collective-permute-done.1), channel_id=1, source_target_pairs={{0,4},{4,8},{8,12},{12,16},{16,20},{20,24},{24,28},{28,0},{1,5},{5... | collective-permute-start | bytes 2752520 | tf_op jit(solution)/shard_map/ppermute | solution.py:43
  463.8 1.0 copy-start.1
  464.8 22.1 %collective-permute-start.3 = (bf16[64,7168]{1,0:T(8,128)(2,1)S(1)}, bf16[64,7168]{1,0:T(8,128)(2,1)S(1)}, u32[]{:S(2)}, u32[]{:S(2)}) collective-permute-start(bf16[64,7168]{1,0:T(8,128)(2,1)S(1)} %collective-permute-done.2), channel_id=1, source_target_pairs={{0,4},{4,8},{8,12},{12,16},{16,20},{20,24},{24,28},{28,0},{1,5},{5... | collective-permute-start | bytes 2752520 | tf_op jit(solution)/shard_map/ppermute | solution.py:43
  486.9 0.9 copy-start.3
  487.8 21.3 %collective-permute-start.4 = (bf16[64,7168]{1,0:T(8,128)(2,1)S(1)}, bf16[64,7168]{1,0:T(8,128)(2,1)S(1)}, u32[]{:S(2)}, u32[]{:S(2)}) collective-permute-start(bf16[64,7168]{1,0:T(8,128)(2,1)S(1)} %collective-permute-done.3), channel_id=1, source_target_pairs={{0,4},{4,8},{8,12},{12,16},{16,20},{20,24},{24,28},{28,0},{1,5},{5... | collective-permute-start | bytes 2752520 | tf_op jit(solution)/shard_map/ppermute | solution.py:43
  509.1 0.9 copy-start.5
  510.0 20.5 %collective-permute-start.5 = (bf16[64,7168]{1,0:T(8,128)(2,1)S(1)}, bf16[64,7168]{1,0:T(8,128)(2,1)}, u32[]{:S(2)}, u32[]{:S(2)}) collective-permute-start(bf16[64,7168]{1,0:T(8,128)(2,1)S(1)} %collective-permute-done.4), channel_id=1, source_target_pairs={{0,4},{4,8},{8,12},{12,16},{16,20},{20,24},{24,28},{28,0},{1,5},{5... | collective-permute-start | bytes 2752520 | tf_op jit(solution)/shard_map/ppermute | solution.py:43
  530.6 19.9 %collective-permute-start.6 = (bf16[64,7168]{1,0:T(8,128)(2,1)}, bf16[64,7168]{1,0:T(8,128)(2,1)}, u32[]{:S(2)}, u32[]{:S(2)}) collective-permute-start(bf16[64,7168]{1,0:T(8,128)(2,1)} %collective-permute-done.5), channel_id=1, source_target_pairs={{0,4},{4,8},{8,12},{12,16},{16,20},{20,24},{24,28},{28,0},{1,5},{5... | collective-permute-start | bytes 2752520 | tf_op jit(solution)/shard_map/ppermute | solution.py:43
  537.1 98.6 %all-to-all-start = ((bf16[512,4,1792]{2,0,1:T(8,128)(2,1)}), bf16[512,4,1792]{2,0,1:T(8,128)(2,1)}, u32[]{:S(2)}, u32[]{:S(2)}) async-start(bf16[512,4,1792]{2,0,1:T(8,128)(2,1)} %bitcast.24), calls=%async_computation.1 | async-start | bytes 14680064 | tf_op jit(solution)/shard_map/all_to_all | solution.py:50
  542.5 99.2 %all-gather.6.cloned.1.call-start = ((), (), s32[]{:S(2)}) async-start(), calls=%async_computation.5 | async-start | bytes 2621440 | tf_op jit(solution)/shard_map/all_gather | solution.py:54
  542.6 26.3 %copy-start.6 = (bf16[64,7168]{1,0:T(8,128)(2,1)S(1)}, bf16[64,7168]{1,0:T(8,128)(2,1)}, u32[]{:S(2)}) copy-start(bf16[64,7168]{1,0:T(8,128)(2,1)} %copy-done.5) | copy-start | bytes 2752516
  542.6 27.2 %copy-start.4 = (bf16[64,7168]{1,0:T(8,128)(2,1)S(1)}, bf16[64,7168]{1,0:T(8,128)(2,1)}, u32[]{:S(2)}) copy-start(bf16[64,7168]{1,0:T(8,128)(2,1)} %copy-done.3) | copy-start | bytes 2752516
  542.6 28.2 %copy-start.2 = (bf16[64,7168]{1,0:T(8,128)(2,1)S(1)}, bf16[64,7168]{1,0:T(8,128)(2,1)}, u32[]{:S(2)}) copy-start(bf16[64,7168]{1,0:T(8,128)(2,1)} %copy-done.1) | copy-start | bytes 2752516
  578.4 3.0 copy-start
  635.7 98.6 %all-to-all-start.1 = ((bf16[512,4,1792]{0,2,1:T(8,128)(2,1)}), bf16[512,4,1792]{0,2,1:T(8,128)(2,1)}, u32[]{:S(2)}, u32[]{:S(2)}) async-start(bf16[512,4,1792]{0,2,1:T(8,128)(2,1)} %bitcast.25), calls=%async_computation.2 | async-start | bytes 14680064 | tf_op jit(solution)/shard_map/all_to_all | solution.py:51
  641.2 103.1 %all-gather.8.cloned.1.call-start = ((), (), s32[]{:S(2)}) async-start(), calls=%async_computation.6 | async-start | bytes 2621440 | tf_op jit(solution)/shard_map/all_gather | solution.py:55
Sparse Core Ops, SparseCore 0:
  10.2 113.9 all-gather.3
  150.8 239.3 reduce-scatter.1
  588.6 31.2 all-gather.5
  643.2 35.7 all-gather.7
